TPU v7x, 32 devices: a whole 2x2x4 slice. The times are simulated.
32 devices in a mesh: dp: 4 (over z), ctx: 4 (over y, x), tensor: 2 (over core).
Axes of the slice: x: 2, y: 2, z: 4, core: 2. Of those that a mesh axis runs over, the one named last changes fastest.
Arguments:
- tokens: bfloat16 [12, 1024, 768], P('dp', 'ctx'), may hold values from -6 to 6
- segment_ids: int32 [12, 1024], P('dp', 'ctx'), may hold values from 0 to 3, never falling along the last dimension, each value on 1 to 512 neighbouring positions
- w_qkv: bfloat16 [3, 768, 768], P(None, None, 'tensor'), may hold values from -0.21875 to 0.21875
- w_out: bfloat16 [768, 768], P('tensor'), may hold values from -3 to 3
- w_up: bfloat16 [3072, 768], P('tensor'), may hold values from -0.21875 to 0.21875
- w_down: bfloat16 [3072, 768], P('tensor'), may hold values from -0.109375 to 0.109375
- norm_gain: float32 [2, 768], replicated, may hold values from 0.1 to 1.9
- norm_bias: float32 [2, 768], replicated, may hold values from -1.5 to 1.5
- grad_out: bfloat16 [12, 1024, 768], P('dp', 'ctx'), may hold values from -6 to 6
Outputs:
- out: bfloat16 [12, 1024, 768], P('dp', 'ctx')
- grad_tokens: float32 [12, 1024, 768], P('dp', 'ctx')
- grad_qkv: float32 [3, 768, 768], P(None, 'ctx', 'tensor')
- grad_w_out: float32 [768, 768], P('tensor', 'ctx')
- grad_up: float32 [3072, 768], P('tensor', 'ctx')
- grad_down: float32 [3072, 768], P('tensor', 'ctx')
- grad_gain: float32 [2, 768], P(None, 'ctx')
- grad_bias: float32 [2, 768], P(None, 'ctx')
Inputs may be any that keep to these rules, and one draw needn't show every extreme that they name: `segment_ids`: documents are contiguous runs of equal ids that never fall along a sequence; each id names 1 to 512 tokens and one document has exactly 512.
All inputs are finite; a program needn't handle non-finite values.
Results may differ from a plain program's by a relative error of at most 0.02.
Values may be sent and summed in bfloat16 or wider, within the bound.
No kernel may reach another device: no remote copies, remote signals or barrier semaphores. Data moves between devices by JAX's collectives and lax.ppermute only.
A program may use at most 320 MiB of HBM per device.

v0:
```python
import jax
import jax.numpy as jnp
from jax import lax
from jax.sharding import PartitionSpec as P

HEAD_DIM = 64
neg_big = -1e30
dims_rows = (((0,), (0,)), ((), ()))
dims_cols = (((1,), (1,)), ((), ()))


def layer_norm(residual, norm_gain, norm_shift):
    center = residual - jnp.mean(residual, axis=-1, keepdims=True)
    spread = jnp.mean(center * center, axis=-1, keepdims=True)
    return center * lax.rsqrt(spread + 1e-06) * norm_gain + norm_shift


def gelu_exact(values):
    return jax.nn.gelu(values, approximate=False)


def scores_of(queries, key_heads):
    return (
        jnp.einsum("sqhd,skhd->shqk", queries, key_heads, preferred_element_type=jnp.float32)
        * 0.125
    )


def score_grads(
    queries, d_heads, lse_query, delta_query, seg_query, key_heads, value_heads, seg_keys
):
    allowed = seg_query[:, None, :, None] == seg_keys[:, None, None, :]
    weights = jnp.where(allowed, jnp.exp(scores_of(queries, key_heads) - lse_query[..., None]), 0.0)
    d_weights = jnp.einsum(
        "sqhd,skhd->shqk", d_heads, value_heads, preferred_element_type=jnp.float32
    )
    d_scores = (weights * (d_weights - delta_query[..., None])).astype(jnp.bfloat16)
    return (weights, d_scores)


def key_grads(queries, d_heads, weights, d_scores):
    grad_keys = (
        jnp.einsum("shqk,sqhd->kshd", d_scores, queries, preferred_element_type=jnp.float32) * 0.125
    )
    grad_values = jnp.einsum(
        "shqk,sqhd->kshd", weights.astype(jnp.bfloat16), d_heads, preferred_element_type=jnp.float32
    )
    return (grad_keys, grad_values)


def on_device(tokens, segment_ids, w_qkv, w_out, w_up, w_down, norm_gain, norm_bias, grad_out):
    seq_count, span_rows, model_width = tokens.shape
    local_width = w_out.shape[0]
    local_heads = local_width // HEAD_DIM
    tok_rows = seq_count * span_rows
    flat_tokens = tokens.reshape(tok_rows, model_width)
    projected = jnp.einsum(
        "tf,jfd->jtd", flat_tokens, w_qkv, preferred_element_type=jnp.float32
    ).astype(jnp.bfloat16)
    queries = projected[0].reshape(seq_count, span_rows, local_heads, HEAD_DIM)
    keys_own = projected[1].reshape(seq_count, span_rows, local_width)
    values_own = projected[2].reshape(seq_count, span_rows, local_width)
    packed = jnp.concatenate([keys_own, values_own], axis=-1)
    full_kv, full_seg = (
        lax.all_gather(packed, "ctx", axis=1, tiled=True),
        lax.all_gather(segment_ids, "ctx", axis=1, tiled=True),
    )
    length = full_seg.shape[1]
    key_block = 1024
    block_count = length // key_block

    def key_piece(step_index):
        offset = step_index * key_block
        kv_piece = lax.dynamic_slice_in_dim(full_kv, offset, key_block, 1).reshape(
            seq_count, key_block, 2, local_heads, HEAD_DIM
        )
        seg_piece = lax.dynamic_slice_in_dim(full_seg, offset, key_block, 1)
        allowed = segment_ids[:, None, :, None] == seg_piece[:, None, None, :]
        return (kv_piece[:, :, 0], kv_piece[:, :, 1], allowed, seg_piece)

    def stats_step(step_index, running):
        row_max, row_sum = running
        key_heads, value_heads, allowed, seg_piece = key_piece(step_index)
        scores = jnp.where(allowed, scores_of(queries, key_heads), neg_big)
        new_max = jnp.maximum(row_max, jnp.max(scores, axis=-1))
        row_sum = row_sum * jnp.exp(row_max - new_max) + jnp.sum(
            jnp.where(allowed, jnp.exp(scores - new_max[..., None]), 0.0), axis=-1
        )
        return (new_max, row_sum)

    stat_shape = (seq_count, local_heads, span_rows)
    row_max, row_sum = lax.fori_loop(
        0,
        block_count,
        stats_step,
        (jnp.full(stat_shape, neg_big, jnp.float32), jnp.zeros(stat_shape, jnp.float32)),
    )
    log_total = row_max + jnp.log(row_sum)

    def mix_step(step_index, running):
        key_heads, value_heads, allowed, seg_piece = key_piece(step_index)
        weights = jnp.where(
            allowed, jnp.exp(scores_of(queries, key_heads) - log_total[..., None]), 0.0
        )
        return running + jnp.einsum(
            "shqk,skhd->sqhd",
            weights.astype(jnp.bfloat16),
            value_heads,
            preferred_element_type=jnp.float32,
        )

    head_shape = (seq_count, span_rows, local_heads, HEAD_DIM)
    mixed_float = lax.fori_loop(0, block_count, mix_step, jnp.zeros(head_shape, jnp.float32))
    mixed_heads = mixed_float.astype(jnp.bfloat16).reshape(tok_rows, local_width)
    attention = lax.psum(
        jnp.dot(mixed_heads, w_out, preferred_element_type=jnp.float32).astype(jnp.bfloat16),
        "tensor",
    ).astype(jnp.float32)
    resid_one = flat_tokens.astype(jnp.float32) + attention
    normed_one = layer_norm(resid_one, norm_gain[0], norm_bias[0])
    normed_low = normed_one.astype(jnp.bfloat16)
    upward = lax.dot_general(normed_low, w_up, dims_cols, preferred_element_type=jnp.float32)
    active = gelu_exact(upward).astype(jnp.bfloat16)
    ffn_out = lax.psum(
        jnp.dot(active, w_down, preferred_element_type=jnp.float32).astype(jnp.bfloat16), "tensor"
    ).astype(jnp.float32)
    resid_two = normed_one + ffn_out
    result, norm_back_two = jax.vjp(layer_norm, resid_two, norm_gain[1], norm_bias[1])
    outputs = result.astype(jnp.bfloat16).reshape(seq_count, span_rows, model_width)
    d_resid_two, d_gain_two, d_bias_two = norm_back_two(
        grad_out.reshape(tok_rows, model_width).astype(jnp.float32)
    )
    d_ffn = d_resid_two.astype(jnp.bfloat16)
    grad_down = lax.dot_general(active, d_ffn, dims_rows, preferred_element_type=jnp.float32)
    d_active = lax.dot_general(d_ffn, w_down, dims_cols, preferred_element_type=jnp.float32)
    gelu_value, gelu_back = jax.vjp(gelu_exact, upward)
    d_up = gelu_back(d_active)[0].astype(jnp.bfloat16)
    grad_up = lax.dot_general(d_up, normed_low, dims_rows, preferred_element_type=jnp.float32)
    d_normed = d_resid_two + lax.psum(
        jnp.dot(d_up, w_up, preferred_element_type=jnp.float32).astype(jnp.bfloat16), "tensor"
    ).astype(jnp.float32)
    norm_value, norm_back_one = jax.vjp(layer_norm, resid_one, norm_gain[0], norm_bias[0])
    d_resid_one, d_gain_one, d_bias_one = norm_back_one(d_normed)
    d_attn = d_resid_one.astype(jnp.bfloat16)
    grad_proj_out = lax.dot_general(
        mixed_heads, d_attn, dims_rows, preferred_element_type=jnp.float32
    )
    d_mixed = (
        lax.dot_general(d_attn, w_out, dims_cols, preferred_element_type=jnp.float32)
        .astype(jnp.bfloat16)
        .reshape(head_shape)
    )
    row_delta = jnp.einsum("sqhd,sqhd->shq", d_mixed.astype(jnp.float32), mixed_float)

    def sender_step(running, step_index):
        key_heads, value_heads, allowed, seg_piece = key_piece(step_index)
        weights, d_scores = score_grads(
            queries, d_mixed, log_total, row_delta, segment_ids, key_heads, value_heads, seg_piece
        )
        running = running + jnp.einsum(
            "shqk,skhd->sqhd", d_scores, key_heads, preferred_element_type=jnp.float32
        )
        grad_keys, grad_values = key_grads(queries, d_mixed, weights, d_scores)
        block_terms = jnp.stack(
            [
                grad_keys.reshape(key_block, seq_count, local_width),
                grad_values.reshape(key_block, seq_count, local_width),
            ],
            axis=2,
        )
        return (running, block_terms)

    query_sum, key_term = lax.scan(
        sender_step, jnp.zeros(head_shape, jnp.float32), jnp.arange(block_count, dtype=jnp.int32)
    )
    key_term = key_term.reshape(length, seq_count, 2, local_width)
    key_grad = lax.psum_scatter(
        key_term.astype(jnp.bfloat16), "ctx", scatter_dimension=0, tiled=True
    ).astype(jnp.float32)
    d_query = (query_sum * 0.125).astype(jnp.bfloat16).reshape(tok_rows, local_width)
    d_keys = key_grad[:, :, 0].astype(jnp.bfloat16)
    d_values = key_grad[:, :, 1].astype(jnp.bfloat16)
    grad_qkv = jnp.stack(
        [
            lax.dot_general(flat_tokens, d_query, dims_rows, preferred_element_type=jnp.float32),
            jnp.einsum("scf,csd->fd", tokens, d_keys, preferred_element_type=jnp.float32),
            jnp.einsum("scf,csd->fd", tokens, d_values, preferred_element_type=jnp.float32),
        ]
    )
    d_query_seq = d_query.reshape(seq_count, span_rows, local_width)
    d_input = (
        jnp.einsum("scd,fd->scf", d_query_seq, w_qkv[0], preferred_element_type=jnp.float32)
        + jnp.einsum("csd,fd->scf", d_keys, w_qkv[1], preferred_element_type=jnp.float32)
        + jnp.einsum("csd,fd->scf", d_values, w_qkv[2], preferred_element_type=jnp.float32)
    )
    grad_tokens = d_resid_one.reshape(seq_count, span_rows, model_width) + lax.psum(
        d_input.astype(jnp.bfloat16), "tensor"
    ).astype(jnp.float32)
    shares = (
        lax.psum_scatter(
            grad_qkv.astype(jnp.bfloat16), "ctx", scatter_dimension=1, tiled=True
        ).astype(jnp.float32),
        lax.psum_scatter(
            grad_proj_out.astype(jnp.bfloat16), "ctx", scatter_dimension=1, tiled=True
        ).astype(jnp.float32),
        lax.psum_scatter(
            grad_up.astype(jnp.bfloat16), "ctx", scatter_dimension=1, tiled=True
        ).astype(jnp.float32),
        lax.psum_scatter(
            grad_down.astype(jnp.bfloat16), "ctx", scatter_dimension=1, tiled=True
        ).astype(jnp.float32),
        lax.psum_scatter(
            jnp.stack([d_gain_one, d_gain_two]).astype(jnp.bfloat16),
            "ctx",
            scatter_dimension=1,
            tiled=True,
        ).astype(jnp.float32),
        lax.psum_scatter(
            jnp.stack([d_bias_one, d_bias_two]).astype(jnp.bfloat16),
            "ctx",
            scatter_dimension=1,
            tiled=True,
        ).astype(jnp.float32),
    )
    totals = (
        lax.psum(shares[0].astype(jnp.bfloat16), "dp").astype(jnp.float32),
        lax.psum(shares[1].astype(jnp.bfloat16), "dp").astype(jnp.float32),
        lax.psum(shares[2].astype(jnp.bfloat16), "dp").astype(jnp.float32),
        lax.psum(shares[3].astype(jnp.bfloat16), "dp").astype(jnp.float32),
        lax.psum(shares[4].astype(jnp.bfloat16), "dp").astype(jnp.float32),
        lax.psum(shares[5].astype(jnp.bfloat16), "dp").astype(jnp.float32),
    )
    return (outputs, grad_tokens, totals[0], totals[1], totals[2], totals[3], totals[4], totals[5])


def solution(mesh):
    return jax.shard_map(
        on_device,
        mesh=mesh,
        in_specs=(
            P("dp", "ctx", None),
            P("dp", "ctx"),
            P(None, None, "tensor"),
            P("tensor", None),
            P("tensor", None),
            P("tensor", None),
            P(),
            P(),
            P("dp", "ctx", None),
        ),
        out_specs=(
            P("dp", "ctx", None),
            P("dp", "ctx", None),
            P(None, "ctx", "tensor"),
            P("tensor", "ctx"),
            P("tensor", "ctx"),
            P("tensor", "ctx"),
            P(None, "ctx"),
            P(None, "ctx"),
        ),
        check_vma=False,
    )
```

profile of v0, /device:TPU:0, one launch (start us, length us, event | category | flops | bytes accessed | tf_op | source)
XLA Modules:
  0.0 660.0 jit_solution(13275955745311117265)
XLA Ops:
  17.3 9.6 %all_gather.7 = s32[3,1024]{1,0:T(4,128)S(1)} all-gather(s32[3,256]{1,0:T(4,128)S(1)} %copy-done.28), channel_id=1, replica_groups=mesh['dp'=4,'ctx'=4,'tensor'=2] {'ctx'}, dimensions={1}, use_global_device_ids=true | all-gather | bytes 15360 | tf_op jit(solution)/shard_map/all_gather | solution.py:66
  27.4 48.7 %all-gather.2.cloned.1.call-done = bf16[3,1024,768]{2,1,0:T(8,128)(2,1)} async-done(((bf16[3,256,768]{2,1,0:T(8,128)(2,1)}), bf16[3,1024,768]{2,1,0:T(8,128)(2,1)}) %all-gather.2.cloned.1.call-update) | async-done | bytes 4718608 | tf_op jit(solution)/shard_map/all_gather | solution.py:65
  76.1 6.7 %copy.50 = bf16[3,1024,768]{1,2,0:T(8,128)(2,1)} copy(bf16[3,1024,768]{2,1,0:T(8,128)(2,1)} %all-gather.2.cloned.1.call-done) | data formatting | bytes 9437184 | tf_op jit(solution)/shard_map/all_gather | solution.py:65
  88.6 6.4 select_reduce_fusion
  95.1 10.0 %bitcast_convert_fusion = (bf16[3,256,6,64]{1,3,2,0:T(8,128)(2,1)S(1)}, f32[3,6,64,256]{3,2,1,0:T(8,128)}) fusion(f32[3,6,256,1024]{3,2,1,0:T(8,128)} %copy-done.2, f32[3,6,256]{2,1,0:T(8,128)S(1)} %log_add_fusion, pred[3,256,1024]{2,1,0:T(8,128)(4,1)S(1)} %broadcast_compare_fusion, bf16[3,1024,2,6,64]{1,4,3,2,0:T(8,128)(2,1)} %bitcast.155), kind=kOutput, calls=%fused_computation.80 | convolution fusion | flops 623149056 | bytes 23808000 | tf_op jit(solution)/shard_map/while/body/eval_jaxpr/shqk,skhd->sqhd/dot_general | solution.py:105
  110.4 18.0 %all-reduce.8.cloned.1.call-done = bf16[768,768]{1,0:T(8,128)(2,1)} async-done(((bf16[768,768]{1,0:T(8,128)(2,1)}), bf16[768,768]{1,0:T(8,128)(2,1)}) %all-reduce.8.cloned.1.call-update) | async-done | bytes 1179664 | tf_op jit(solution)/shard_map/psum | solution.py:115
  130.9 15.0 %multiply_convert_fusion.2 = (bf16[768,1536]{1,0:T(8,128)(2,1)S(1)}, f32[768,1536]{1,0:T(8,128)}, f32[768,1536]{1,0:T(8,128)}) fusion(bf16[1536,768]{1,0:T(8,128)(2,1)S(1)} %copy-done, f32[768,768]{1,0:T(8,128)S(1)} %get-tuple-element.134, f32[768]{0:T(1024)S(1)} %copy-done.30, f32[768]{0:T(1024)S(1)} %get-tuple-element.144, f32[768]{0:T(1024)S(1)} %fusion.46), kind=kOutput, calls=%fused_computation.10 | convolution fusion | flops 1890975744 | bytes 16524288 | tf_op jit(solution)/shard_map/dot_general | solution.py:122
  150.4 21.1 %all-reduce.10.cloned.1.call-done = bf16[768,768]{1,0:T(8,128)(2,1)} async-done(((bf16[768,768]{1,0:T(8,128)(2,1)}), bf16[768,768]{1,0:T(8,128)(2,1)}) %all-reduce.10.cloned.1.call-update) | async-done | bytes 1179664 | tf_op jit(solution)/shard_map/psum | solution.py:124
  179.2 6.5 add_convert_fusion
  190.4 20.9 %all-reduce.12.cloned.1.call-done = bf16[768,768]{1,0:T(8,128)(2,1)} async-done(((bf16[768,768]{1,0:T(8,128)(2,1)}), bf16[768,768]{1,0:T(8,128)(2,1)}) %all-reduce.12.cloned.1.call-update) | async-done | bytes 1179664 | tf_op jit(solution)/shard_map/psum | solution.py:139
  223.8 12.2 %convolution_convert_fusion.2 = bf16[3,6,64,1024]{3,2,1,0:T(8,128)(2,1)} fusion(bf16[3,256,6,64]{1,0,3,2:T(4,128)(2,1)} %reshape.160, f32[3,6,256,1024]{3,2,1,0:T(8,128)} %copy-done.2, f32[3,6,256]{2,1,0:T(8,128)S(1)} %copy-done.25, pred[3,256,1024]{2,1,0:T(8,128)(4,1)} %copy-done.10), kind=kOutput, calls=%fused_computation.55 | convolution fusion | flops 624033792 | bytes 22628352 | tf_op jit(solution)/shard_map/while/body/eval_jaxpr/shqk,sqhd->kshd/dot_general | solution.py:45
  236.2 13.0 %multiply_convert_fusion = bf16[3,6,256,1024]{3,2,1,0:T(8,128)(2,1)} fusion(f32[3,6,256,1024]{3,2,1,0:T(8,128)} %copy-done.2, f32[3,6,256]{2,1,0:T(8,128)S(1)} %fusion.25, f32[3,6,256]{2,1,0:T(8,128)S(1)} %copy-done.25, pred[3,256,1024]{2,1,0:T(8,128)(4,1)} %copy-done.10, bf16[3,1024,2,6,64]{1,4,3,2,0:T(8,128)(2,1)S(1)} %bitcast.159, ...), kind=kOutput, calls=%fused_computation | convolution fusion | flops 632291328 | bytes 32096256 | tf_op jit(solution)/shard_map/while/body/eval_jaxpr/sqhd,skhd->shqk/dot_general | solution.py:34
  249.3 7.1 %multiply_convert_fusion.1 = bf16[3,6,64,1024]{3,2,1,0:T(8,128)(2,1)} fusion(bf16[3,6,256,1024]{3,2,1,0:T(8,128)(2,1)} %multiply_convert_fusion, bf16[3,256,6,64]{1,0,3,2:T(4,128)(2,1)} %reshape_squeeze.11), kind=kOutput, calls=%fused_computation.8 | convolution fusion | flops 606339072 | bytes 12386304 | tf_op jit(solution)/shard_map/while/body/eval_jaxpr/shqk,sqhd->kshd/dot_general | solution.py:43
  270.3 7.4 %fusion.19 = bf16[3,6,64,256]{3,2,1,0:T(8,128)(2,1)S(1)} fusion(bf16[3,6,256,1024]{3,2,1,0:T(8,128)(2,1)} %multiply_convert_fusion, bf16[3,1024,2,6,64]{1,4,3,2,0:T(8,128)(2,1)} %bitcast.156), kind=kOutput, calls=%fused_computation.66 | convolution fusion | flops 604569600 | bytes 12386304 | tf_op jit(solution)/shard_map/while/body/eval_jaxpr/shqk,skhd->sqhd/dot_general | solution.py:160
  279.8 48.6 %reduce-scatter.14.cloned.1.call-done = bf16[256,3,2,384]{3,0,1,2:T(8,128)(2,1)} async-done(((bf16[1024,3,2,384]{3,0,1,2:T(8,128)(2,1)}), bf16[256,3,2,384]{3,0,1,2:T(8,128)(2,1)}) %reduce-scatter.14.cloned.1.call-update) | async-done | bytes 1179664 | tf_op jit(solution)/shard_map/reduce_scatter | solution.py:177
  367.5 6.4 reduce-scatter.22.cloned.1.call-done
  376.6 26.1 %reduce-scatter.16.cloned.1.call-done = bf16[384,192]{0,1:T(8,128)(2,1)} async-done(((bf16[384,768]{0,1:T(8,128)(2,1)}), bf16[384,192]{0,1:T(8,128)(2,1)}) %reduce-scatter.16.cloned.1.call-update) | async-done | bytes 147472 | tf_op jit(solution)/shard_map/reduce_scatter | solution.py:203
  402.7 40.4 %reduce-scatter.20.cloned.1.call-done = bf16[1536,192]{0,1:T(8,128)(2,1)} async-done(((bf16[1536,768]{0,1:T(8,128)(2,1)}), bf16[1536,192]{0,1:T(8,128)(2,1)}) %reduce-scatter.20.cloned.1.call-update) | async-done | bytes 589840 | tf_op jit(solution)/shard_map/reduce_scatter | solution.py:209
  443.2 40.5 %reduce-scatter.18.cloned.1.call-done = bf16[1536,192]{0,1:T(8,128)(2,1)} async-done(((bf16[1536,768]{0,1:T(8,128)(2,1)}), bf16[1536,192]{0,1:T(8,128)(2,1)}) %reduce-scatter.18.cloned.1.call-update) | async-done | bytes 589840 | tf_op jit(solution)/shard_map/reduce_scatter | solution.py:206
  483.7 27.2 %reduce-scatter.24.cloned.1.call-done = bf16[192,2]{1,0:T(8,128)(2,1)} async-done(((bf16[768,2]{1,0:T(8,128)(2,1)}), bf16[192,2]{1,0:T(8,128)(2,1)}) %reduce-scatter.24.cloned.1.call-update) | async-done | bytes 784
  511.7 25.9 %reduce-scatter.26.cloned.1.call-done = bf16[192,2]{1,0:T(8,128)(2,1)} async-done(((bf16[768,2]{1,0:T(8,128)(2,1)}), bf16[192,2]{1,0:T(8,128)(2,1)}) %reduce-scatter.26.cloned.1.call-update) | async-done | bytes 784
  538.5 11.7 %all-reduce = (bf16[2,192]{1,0:T(2,128)(2,1)S(1)}, bf16[2,192]{1,0:T(2,128)(2,1)S(1)}) all-reduce(bf16[2,192]{1,0:T(2,128)(2,1)S(1)} %copy.79, bf16[2,192]{1,0:T(2,128)(2,1)S(1)} %copy.81), channel_id=1, replica_groups=mesh['dp'=4,'ctx'=4,'tensor'=2] {'dp'}, use_global_device_ids=true, to_apply=%region_26.27 | all-reduce | flops 768 | bytes 3072 | tf_op jit(solution)/shard_map/psum | solution.py:230
  551.4 8.9 %all-reduce.14.cloned.1.call-done = bf16[3,256,768]{2,1,0:T(8,128)(2,1)} async-done(((bf16[3,256,768]{2,1,0:T(8,128)(2,1)}), bf16[3,256,768]{2,1,0:T(8,128)(2,1)}) %all-reduce.14.cloned.1.call-update) | async-done | bytes 1179664 | tf_op jit(solution)/shard_map/psum | solution.py:196
  563.1 83.4 %all-reduce.16.cloned.1.call-done = (bf16[3,192,384]{1,2,0:T(8,128)(2,1)}, bf16[384,192]{0,1:T(8,128)(2,1)}, bf16[1536,192]{0,1:T(8,128)(2,1)}, bf16[1536,192]{0,1:T(8,128)(2,1)}) async-done(((bf16[3,192,384]{1,2,0:T(8,128)(2,1)}, bf16[384,192]{0,1:T(8,128)(2,1)}, bf16[1536,192]{0,1:T(8,128)(2,1)}, bf16[1536,192]{0,1:T(8,128)(2,1)}), (bf16[3,192,384]{1,2,0:T(8,128)(2,1)}, bf16[384,192]{0,1:T(8,128)(2,1)}, ...) | async-done | bytes 1769488 | tf_op jit(solution)/shard_map/psum | solution.py:226
  (184 shorter events, 123.3 us)
Async XLA Ops:
  7.2 123.7 %copy-start = (bf16[1536,768]{1,0:T(8,128)(2,1)S(1)}, bf16[1536,768]{1,0:T(8,128)(2,1)}, u32[]{:S(2)}) copy-start(bf16[1536,768]{1,0:T(8,128)(2,1)} %param.13) | copy-start | bytes 7077892
  7.2 68.9 %all-gather.2.cloned.1.call-start = ((), (), s32[]{:S(2)}) async-start(), calls=%async_computation.7 | async-start | bytes 5898240 | tf_op jit(solution)/shard_map/all_gather | solution.py:65
  16.2 112.2 %all-reduce.8.cloned.1.call-start = ((), (), s32[]{:S(2)}) async-start(), calls=%async_computation.8 | async-start | bytes 2359296 | tf_op jit(solution)/shard_map/psum | solution.py:115
  27.4 67.6 %copy-start.10 = (pred[3,256,1024]{2,1,0:T(8,128)(4,1)}, pred[3,256,1024]{2,1,0:T(8,128)(4,1)S(1)}, u32[]{:S(2)}) copy-start(pred[3,256,1024]{2,1,0:T(8,128)(4,1)S(1)} %broadcast_compare_fusion) | copy-start | bytes 2359300
  105.6 22.8 %copy-start.11 = (bf16[3,256,768]{2,1,0:T(8,128)(2,1)S(1)}, bf16[3,256,768]{2,1,0:T(8,128)(2,1)}, u32[]{:S(2)}) copy-start(bf16[3,256,768]{2,1,0:T(8,128)(2,1)} %param.9) | copy-start | bytes 3538948
  108.4 63.0 %all-reduce.10.cloned.1.call-start = ((), (), s32[]{:S(2)}) async-start(), calls=%async_computation.9 | async-start | bytes 2359296 | tf_op jit(solution)/shard_map/psum | solution.py:124
  130.8 15.1 %copy-start.3 = (f32[768,768]{1,0:T(8,128)}, f32[768,768]{1,0:T(8,128)S(1)}, u32[]{:S(2)}) copy-start(f32[768,768]{1,0:T(8,128)S(1)} %get-tuple-element.134) | copy-start | bytes 7077892
  130.9 16.4 %copy-start.35 = (bf16[1536,768]{1,0:T(8,128)(2,1)S(1)}, bf16[1536,768]{1,0:T(8,128)(2,1)}, u32[]{:S(2)}) copy-start(bf16[1536,768]{1,0:T(8,128)(2,1)} %param.14) | copy-start | bytes 7077892
  147.3 24.2 %copy-start.31 = (f32[768]{0:T(1024)S(1)}, f32[768]{0:T(1024)}, u32[]{:S(2)}) copy-start(f32[768]{0:T(1024)} %get-tuple-element.119) | copy-start | bytes 9220
  150.3 61.0 %all-reduce.12.cloned.1.call-start = ((), (), s32[]{:S(2)}) async-start(), calls=%async_computation.10 | async-start | bytes 2359296 | tf_op jit(solution)/shard_map/psum | solution.py:139
  179.2 32.1 %copy-start.26 = (f32[768]{0:T(1024)}, f32[768]{0:T(1024)S(1)}, u32[]{:S(2)}) copy-start(f32[768]{0:T(1024)S(1)} %negate_multiply_fusion.2) | copy-start | bytes 9220
  190.2 25.3 %copy-start.4 = (f32[768,768]{1,0:T(8,128)S(1)}, f32[768,768]{1,0:T(8,128)}, u32[]{:S(2)}) copy-start(f32[768,768]{1,0:T(8,128)} %copy-done.3) | copy-start | bytes 7077892
  190.2 138.3 %reduce-scatter.14.cloned.1.call-start = ((), (), s32[]{:S(2)}) async-start(), calls=%async_computation.11 | async-start | bytes 5898240 | tf_op jit(solution)/shard_map/reduce_scatter | solution.py:177
  219.3 17.0 %slice-start = ((s8[4718592]{0:T(1024)(128)(4,1)}), s8[524288]{0:T(1024)(128)(4,1)S(1)}, s32[]{:S(2)}) async-start(s8[4718592]{0:T(1024)(128)(4,1)} %bitcast.157), calls=%async_computation.20 | async-start | bytes 1048576
  223.7 12.5 %slice-start.1 = ((s8[4718592]{0:T(1024)(128)(4,1)}), s8[4194304]{0:T(1024)(128)(4,1)S(1)}, s32[]{:S(2)}) async-start(s8[4718592]{0:T(1024)(128)(4,1)} %bitcast.157), calls=%async_computation.21 | async-start | bytes 8388608
  270.1 103.9 %reduce-scatter.22.cloned.1.call-start = ((), (), s32[]{:S(2)}) async-start(), calls=%async_computation.16 | async-start | bytes 2211840
  341.3 61.4 %reduce-scatter.16.cloned.1.call-start = ((), (), s32[]{:S(2)}) async-start(), calls=%async_computation.13 | async-start | bytes 737280 | tf_op jit(solution)/shard_map/reduce_scatter | solution.py:203
  344.7 98.4 %reduce-scatter.20.cloned.1.call-start = ((), (), s32[]{:S(2)}) async-start(), calls=%async_computation.15 | async-start | bytes 2949120 | tf_op jit(solution)/shard_map/reduce_scatter | solution.py:209
  350.7 132.9 %reduce-scatter.18.cloned.1.call-start = ((), (), s32[]{:S(2)}) async-start(), calls=%async_computation.14 | async-start | bytes 2949120 | tf_op jit(solution)/shard_map/reduce_scatter | solution.py:206
  356.7 154.2 %reduce-scatter.24.cloned.1.call-start = ((), (), s32[]{:S(2)}) async-start(), calls=%async_computation.17 | async-start | bytes 245760
  359.1 178.5 %reduce-scatter.26.cloned.1.call-start = ((), (), s32[]{:S(2)}) async-start(), calls=%async_computation.18 | async-start | bytes 245760
  360.1 200.2 %all-reduce.14.cloned.1.call-start = ((), (), s32[]{:S(2)}) async-start(), calls=%async_computation.12 | async-start | bytes 2359296 | tf_op jit(solution)/shard_map/psum | solution.py:196
  367.5 192.8 %copy-start.6 = (f32[768,768]{1,0:T(8,128)S(1)}, f32[768,768]{1,0:T(8,128)}, u32[]{:S(2)}) copy-start(f32[768,768]{1,0:T(8,128)} %copy-done.5) | copy-start | bytes 7077892
  367.5 279.1 %all-reduce.16.cloned.1.call-start = ((), (), s32[]{:S(2)}) async-start(), calls=%async_computation.19 | async-start | bytes 3833856 | tf_op jit(solution)/shard_map/psum | solution.py:226
  (30 other events, 99.0 us)
Sparse Core Ops, SparseCore 0:
  16.3 59.7 all-gather.1
  108.6 19.7 all-reduce.7
  150.5 20.9 all-reduce.9
  190.3 20.9 all-reduce.11
  270.2 58.2 reduce-scatter.13
  341.4 32.4 reduce-scatter.21
  377.6 25.0 reduce-scatter.15
  405.8 37.3 reduce-scatter.19
  446.2 37.3 reduce-scatter.17
  486.8 23.9 reduce-scatter.23
  513.6 23.9 reduce-scatter.25
  540.4 19.7 all-reduce.13
  563.6 82.8 all-reduce.15
where the time goes:
time: 669 us; the launch traced here: 660 us
  waiting for transfers between devices  416 us (62%)
  matrix products  114 us (17%)
  local copies, waits for them, and re-layouts  49.5 us (7%)
  other arithmetic  41.9 us (6%)
  blocking collectives  21.3 us (3%)
  between operations  14.9 us (2%)
    psum x1, waiting for transfers between devices, on_device(): lax.psum(shares[0].astype(jnp.bfloat16), 'dp').astype(jnp.float32)  83.4 us
    unnamed x16, waiting for transfers between devices  59.7 us
    all_gather x1, waiting for transfers between devices, on_device(): lax.all_gather(packed, 'ctx', axis=1, tiled=True)  48.7 us
    reduce_scatter x1, waiting for transfers between devices, on_device(): lax.psum_scatter(key_term.astype(jnp.bfloat16), 'ctx', scatter_dimension=...  48.6 us
    reduce_scatter x1, waiting for transfers between devices, on_device(): lax.psum_scatter(grad_up.astype(jnp.bfloat16), 'ctx', scatter_dimension=1...  40.5 us
    reduce_scatter x1, waiting for transfers between devices, on_device(): lax.psum_scatter(grad_down.astype(jnp.bfloat16), 'ctx', scatter_dimension...  40.4 us
    reduce_scatter x1, waiting for transfers between devices, on_device(): lax.psum_scatter(grad_proj_out.astype(jnp.bfloat16), 'ctx', scatter_dimen...  26.1 us
    unnamed x93, local copies, waits for them, and re-layouts  24.6 us
  transfers between devices with their start and end apart: 13, of which 13 were waited for; matrix products, arithmetic and copies ran while one was open for 7% of the time, Pallas kernels for 0%

commit v1 on v0

--- a/solution.py
+++ b/solution.py
@@ -49,6 +49,25 @@
 
 
 def on_device(tokens, segment_ids, w_qkv, w_out, w_up, w_down, norm_gain, norm_bias, grad_out):
+
+    def fix_pages_by_axis(body, ax_name, array_axis):
+        size_here = lax.axis_size(ax_name)
+        history = tuple(((rr, (rr + 1) % size_here) for rr in range(size_here)))
+        crops = tuple(((rr, (rr - 1) % size_here) for rr in range(size_here)))
+        z2, out_arr = ([body], [body])
+        for _ in range(size_here // 2):
+            z2.append(lax.ppermute(z2[-1], axis_name=ax_name, perm=history))
+        for _ in [*range((size_here - 1) // 2)]:
+            val = lax.ppermute(out_arr[-1], axis_name=ax_name, perm=crops)
+            out_arr.append(val)
+        built = jnp.concatenate([*z2[::-1], *out_arr[1:]], axis=array_axis)
+        carry_out = jnp.roll(
+            built,
+            shift=(lax.axis_index(ax_name) - size_here // 2) * body.shape[array_axis],
+            axis=array_axis,
+        )
+        return carry_out
+
     seq_count, span_rows, model_width = tokens.shape
     local_width = w_out.shape[0]
     local_heads = local_width // HEAD_DIM
@@ -62,7 +81,7 @@
     values_own = projected[2].reshape(seq_count, span_rows, local_width)
     packed = jnp.concatenate([keys_own, values_own], axis=-1)
     full_kv, full_seg = (
-        lax.all_gather(packed, "ctx", axis=1, tiled=True),
+        fix_pages_by_axis(packed, "ctx", 1),
         lax.all_gather(segment_ids, "ctx", axis=1, tiled=True),
     )
     length = full_seg.shape[1]

time: 669 us -> 701 us (1.048)
  blocking collectives: 21.3 us -> 61.9 us
  waiting for transfers between devices: 416 us -> 395 us
  local copies, waits for them, and re-layouts: 49.5 us -> 61.8 us
    all_gather x1 -> x0, waiting for transfers between devices: 48.7 us -> none  [on_device(): lax.all_gather(packed, 'ctx', axis=1, tiled=True)]
    all_gather x1, blocking collectives: 9.6 us -> 50.2 us  [on_device(): lax.all_gather(segment_ids, 'ctx', axis=1, tiled=True)]
    ppermute x0 -> x3, waiting for transfers between devices: none -> 27.2 us  [the longest x2 27.2 us: fix_pages_by_axis(): z2.append(lax.ppermute(z2[-1], axis_name=ax_name, perm=history))]
    dynamic_slice x0 -> x2, local copies, waits for them, and re-layouts: none -> 9.16 us  [fix_pages_by_axis(): jnp.roll(built, shift=(lax.axis_index(ax_name) - size_here // 2) * body.s...]
    unnamed x93 -> x100, local copies, waits for them, and re-layouts: 24.6 us -> 31.7 us
    unnamed x16 -> x15, waiting for transfers between devices: 59.7 us -> 60.2 us
  transfers between devices with their start and end apart: 13 -> 15, of which waited for: 13 -> 13; matrix products, arithmetic and copies ran while one was open for 7% -> 7% of each run, Pallas kernels for 0% -> 0%
where the time goes in v1:
time: 701 us; the launch traced here: 697 us
  waiting for transfers between devices  395 us (56%)
  matrix products  113 us (16%)
  blocking collectives  61.9 us (9%)
  local copies, waits for them, and re-layouts  61.8 us (9%)
  other arithmetic  42.8 us (6%)
  between operations  15 us (2%)
  starting transfers between devices  7.33 us (1%)
    psum x1, waiting for transfers between devices, on_device(): lax.psum(shares[0].astype(jnp.bfloat16), 'dp').astype(jnp.float32)  82.6 us
    unnamed x15, waiting for transfers between devices  60.2 us
    all_gather x1, blocking collectives, on_device(): lax.all_gather(segment_ids, 'ctx', axis=1, tiled=True)  50.2 us
    reduce_scatter x1, waiting for transfers between devices, on_device(): lax.psum_scatter(key_term.astype(jnp.bfloat16), 'ctx', scatter_dimension=...  47.6 us
    reduce_scatter x1, waiting for transfers between devices, on_device(): lax.psum_scatter(grad_up.astype(jnp.bfloat16), 'ctx', scatter_dimension=1...  40.5 us
    reduce_scatter x1, waiting for transfers between devices, on_device(): lax.psum_scatter(grad_down.astype(jnp.bfloat16), 'ctx', scatter_dimension...  40.5 us
    unnamed x100, local copies, waits for them, and re-layouts  31.7 us
    ppermute x2, waiting for transfers between devices, fix_pages_by_axis(): z2.append(lax.ppermute(z2[-1], axis_name=ax_name, perm=history))  27.2 us
  transfers between devices with their start and end apart: 15, of which 13 were waited for; matrix products, arithmetic and copies ran while one was open for 7% of the time, Pallas kernels for 0%

profile of v1, /device:TPU:0, one launch (start us, length us, event | category | flops | bytes accessed | tf_op | source)
XLA Modules:
  0.0 697.2 jit_solution(17883349498684183213)
XLA Ops:
  17.6 27.2 %collective-permute-done = bf16[3,256,768]{2,1,0:T(8,128)(2,1)} collective-permute-done((bf16[3,256,768]{2,1,0:T(8,128)(2,1)}, bf16[3,256,768]{2,1,0:T(8,128)(2,1)}, u32[]{:S(2)}, u32[]{:S(2)}) %collective-permute-start) | collective-permute-done | bytes 1179680 | tf_op jit(solution)/shard_map/ppermute | solution.py:59
  49.8 50.2 %all_gather.3 = s32[3,1024]{1,0:T(4,128)S(1)} all-gather(s32[3,256]{1,0:T(4,128)S(1)} %copy-done.29), channel_id=1, replica_groups=mesh['dp'=4,'ctx'=4,'tensor'=2] {'ctx'}, dimensions={1}, use_global_device_ids=true | all-gather | bytes 15360 | tf_op jit(solution)/shard_map/all_gather | solution.py:85
  112.1 6.7 copy.50
  124.7 6.4 select_reduce_fusion
  131.2 10.0 %bitcast_convert_fusion = (bf16[3,256,6,64]{1,3,2,0:T(8,128)(2,1)S(1)}, f32[3,6,64,256]{3,2,1,0:T(8,128)}) fusion(f32[3,6,256,1024]{3,2,1,0:T(8,128)} %copy-done.1, f32[3,6,256]{2,1,0:T(8,128)S(1)} %log_add_fusion, pred[3,256,1024]{2,1,0:T(8,128)(4,1)S(1)} %copy-done.8, bf16[3,1024,2,6,64]{1,4,3,2,0:T(8,128)(2,1)} %bitcast.155), kind=kOutput, calls=%fused_computation.80 | convolution fusion | flops 623149056 | bytes 23808000 | tf_op jit(solution)/shard_map/while/body/eval_jaxpr/shqk,skhd->sqhd/dot_general | solution.py:124
  146.1 19.4 %all-reduce.8.cloned.1.call-done = bf16[768,768]{1,0:T(8,128)(2,1)} async-done(((bf16[768,768]{1,0:T(8,128)(2,1)}), bf16[768,768]{1,0:T(8,128)(2,1)}) %all-reduce.8.cloned.1.call-update) | async-done | bytes 1179664 | tf_op jit(solution)/shard_map/psum | solution.py:134
  168.0 15.1 %multiply_convert_fusion.2 = (bf16[768,1536]{1,0:T(8,128)(2,1)S(1)}, f32[768,1536]{1,0:T(8,128)}, f32[768,1536]{1,0:T(8,128)}) fusion(bf16[1536,768]{1,0:T(8,128)(2,1)S(1)} %copy-done, f32[768,768]{1,0:T(8,128)S(1)} %get-tuple-element.134, f32[768]{0:T(1024)S(1)} %copy-done.31, f32[768]{0:T(1024)S(1)} %get-tuple-element.144, f32[768]{0:T(1024)S(1)} %fusion.46), kind=kOutput, calls=%fused_computation.10 | convolution fusion | flops 1890975744 | bytes 16524288 | tf_op jit(solution)/shard_map/dot_general | solution.py:141
  187.6 21.1 %all-reduce.10.cloned.1.call-done = bf16[768,768]{1,0:T(8,128)(2,1)} async-done(((bf16[768,768]{1,0:T(8,128)(2,1)}), bf16[768,768]{1,0:T(8,128)(2,1)}) %all-reduce.10.cloned.1.call-update) | async-done | bytes 1179664 | tf_op jit(solution)/shard_map/psum | solution.py:143
  216.4 6.5 add_convert_fusion
  227.7 20.9 %all-reduce.12.cloned.1.call-done = bf16[768,768]{1,0:T(8,128)(2,1)} async-done(((bf16[768,768]{1,0:T(8,128)(2,1)}), bf16[768,768]{1,0:T(8,128)(2,1)}) %all-reduce.12.cloned.1.call-update) | async-done | bytes 1179664 | tf_op jit(solution)/shard_map/psum | solution.py:158
  260.8 12.2 %convolution_convert_fusion.2 = bf16[3,6,64,1024]{3,2,1,0:T(8,128)(2,1)} fusion(bf16[3,256,6,64]{1,0,3,2:T(4,128)(2,1)} %reshape.160, f32[3,6,256,1024]{3,2,1,0:T(8,128)} %copy-done.1, f32[3,6,256]{2,1,0:T(8,128)S(1)} %copy-done.26, pred[3,256,1024]{2,1,0:T(8,128)(4,1)} %broadcast_compare_fusion), kind=kOutput, calls=%fused_computation.55 | convolution fusion | flops 624033792 | bytes 22628352 | tf_op jit(solution)/shard_map/while/body/eval_jaxpr/shqk,sqhd->kshd/dot_general | solution.py:45
  273.3 13.0 %multiply_convert_fusion = bf16[3,6,256,1024]{3,2,1,0:T(8,128)(2,1)} fusion(f32[3,6,256,1024]{3,2,1,0:T(8,128)} %copy-done.1, f32[3,6,256]{2,1,0:T(8,128)S(1)} %fusion.25, f32[3,6,256]{2,1,0:T(8,128)S(1)} %copy-done.26, pred[3,256,1024]{2,1,0:T(8,128)(4,1)} %broadcast_compare_fusion, bf16[3,1024,2,6,64]{1,4,3,2,0:T(8,128)(2,1)S(1)} %bitcast.159, ...), kind=kOutput, calls=%fused_computation | convolution fusion | flops 632291328 | bytes 32096256 | tf_op jit(solution)/shard_map/while/body/eval_jaxpr/sqhd,skhd->shqk/dot_general | solution.py:34
  286.4 7.2 %multiply_convert_fusion.1 = bf16[3,6,64,1024]{3,2,1,0:T(8,128)(2,1)} fusion(bf16[3,6,256,1024]{3,2,1,0:T(8,128)(2,1)} %multiply_convert_fusion, bf16[3,256,6,64]{1,0,3,2:T(4,128)(2,1)} %reshape_squeeze.11), kind=kOutput, calls=%fused_computation.8 | convolution fusion | flops 606339072 | bytes 12386304 | tf_op jit(solution)/shard_map/while/body/eval_jaxpr/shqk,sqhd->kshd/dot_general | solution.py:43
  307.7 7.4 %fusion.19 = bf16[3,6,64,256]{3,2,1,0:T(8,128)(2,1)S(1)} fusion(bf16[3,6,256,1024]{3,2,1,0:T(8,128)(2,1)} %multiply_convert_fusion, bf16[3,1024,2,6,64]{1,4,3,2,0:T(8,128)(2,1)} %bitcast.156), kind=kOutput, calls=%fused_computation.66 | convolution fusion | flops 604569600 | bytes 12386304 | tf_op jit(solution)/shard_map/while/body/eval_jaxpr/shqk,skhd->sqhd/dot_general | solution.py:179
  318.1 47.6 %reduce-scatter.14.cloned.1.call-done = bf16[256,3,2,384]{3,0,1,2:T(8,128)(2,1)} async-done(((bf16[1024,3,2,384]{3,0,1,2:T(8,128)(2,1)}), bf16[256,3,2,384]{3,0,1,2:T(8,128)(2,1)}) %reduce-scatter.14.cloned.1.call-update) | async-done | bytes 1179664 | tf_op jit(solution)/shard_map/reduce_scatter | solution.py:196
  404.3 6.3 reduce-scatter.22.cloned.1.call-done
  413.4 25.9 %reduce-scatter.16.cloned.1.call-done = bf16[384,192]{0,1:T(8,128)(2,1)} async-done(((bf16[384,768]{0,1:T(8,128)(2,1)}), bf16[384,192]{0,1:T(8,128)(2,1)}) %reduce-scatter.16.cloned.1.call-update) | async-done | bytes 147472 | tf_op jit(solution)/shard_map/reduce_scatter | solution.py:222
  439.3 40.5 %reduce-scatter.20.cloned.1.call-done = bf16[1536,192]{0,1:T(8,128)(2,1)} async-done(((bf16[1536,768]{0,1:T(8,128)(2,1)}), bf16[1536,192]{0,1:T(8,128)(2,1)}) %reduce-scatter.20.cloned.1.call-update) | async-done | bytes 589840 | tf_op jit(solution)/shard_map/reduce_scatter | solution.py:228
  479.8 40.5 %reduce-scatter.18.cloned.1.call-done = bf16[1536,192]{0,1:T(8,128)(2,1)} async-done(((bf16[1536,768]{0,1:T(8,128)(2,1)}), bf16[1536,192]{0,1:T(8,128)(2,1)}) %reduce-scatter.18.cloned.1.call-update) | async-done | bytes 589840 | tf_op jit(solution)/shard_map/reduce_scatter | solution.py:225
  520.3 27.3 %reduce-scatter.24.cloned.1.call-done = bf16[192,2]{1,0:T(8,128)(2,1)} async-done(((bf16[768,2]{1,0:T(8,128)(2,1)}), bf16[192,2]{1,0:T(8,128)(2,1)}) %reduce-scatter.24.cloned.1.call-update) | async-done | bytes 784
  548.5 26.3 %reduce-scatter.26.cloned.1.call-done = bf16[192,2]{1,0:T(8,128)(2,1)} async-done(((bf16[768,2]{1,0:T(8,128)(2,1)}), bf16[192,2]{1,0:T(8,128)(2,1)}) %reduce-scatter.26.cloned.1.call-update) | async-done | bytes 784
  575.7 11.7 %all-reduce = (bf16[2,192]{1,0:T(2,128)(2,1)S(1)}, bf16[2,192]{1,0:T(2,128)(2,1)S(1)}) all-reduce(bf16[2,192]{1,0:T(2,128)(2,1)S(1)} %copy.79, bf16[2,192]{1,0:T(2,128)(2,1)S(1)} %copy.81), channel_id=1, replica_groups=mesh['dp'=4,'ctx'=4,'tensor'=2] {'dp'}, use_global_device_ids=true, to_apply=%region_26.27 | all-reduce | flops 768 | bytes 3072 | tf_op jit(solution)/shard_map/psum | solution.py:249
  588.5 9.0 %all-reduce.14.cloned.1.call-done = bf16[3,256,768]{2,1,0:T(8,128)(2,1)} async-done(((bf16[3,256,768]{2,1,0:T(8,128)(2,1)}), bf16[3,256,768]{2,1,0:T(8,128)(2,1)}) %all-reduce.14.cloned.1.call-update) | async-done | bytes 1179664 | tf_op jit(solution)/shard_map/psum | solution.py:215
  601.2 82.6 %all-reduce.16.cloned.1.call-done = (bf16[3,192,384]{1,2,0:T(8,128)(2,1)}, bf16[384,192]{0,1:T(8,128)(2,1)}, bf16[1536,192]{0,1:T(8,128)(2,1)}, bf16[1536,192]{0,1:T(8,128)(2,1)}) async-done(((bf16[3,192,384]{1,2,0:T(8,128)(2,1)}, bf16[384,192]{0,1:T(8,128)(2,1)}, bf16[1536,192]{0,1:T(8,128)(2,1)}, bf16[1536,192]{0,1:T(8,128)(2,1)}), (bf16[3,192,384]{1,2,0:T(8,128)(2,1)}, bf16[384,192]{0,1:T(8,128)(2,1)}, ...) | async-done | bytes 1769488 | tf_op jit(solution)/shard_map/psum | solution.py:245
  (198 shorter events, 141.0 us)
Async XLA Ops:
  7.2 160.8 %copy-start = (bf16[1536,768]{1,0:T(8,128)(2,1)S(1)}, bf16[1536,768]{1,0:T(8,128)(2,1)}, u32[]{:S(2)}) copy-start(bf16[1536,768]{1,0:T(8,128)(2,1)} %param.13) | copy-start | bytes 7077892
  7.2 158.4 %all-reduce.8.cloned.1.call-start = ((), (), s32[]{:S(2)}) async-start(), calls=%async_computation.7 | async-start | bytes 2359296 | tf_op jit(solution)/shard_map/psum | solution.py:134
  12.2 37.6 %copy-start.29 = (s32[3,256]{1,0:T(4,128)S(1)}, s32[3,256]{1,0:T(4,128)}, u32[]{:S(2)}) copy-start(s32[3,256]{1,0:T(4,128)} %param.10) | copy-start | bytes 9220
  14.7 30.2 %collective-permute-start = (bf16[3,256,768]{2,1,0:T(8,128)(2,1)}, bf16[3,256,768]{2,1,0:T(8,128)(2,1)}, u32[]{:S(2)}, u32[]{:S(2)}) collective-permute-start(bf16[3,256,768]{2,1,0:T(8,128)(2,1)} %pad_maximum_fusion.2), channel_id=1, source_target_pairs={{0,2},{2,4},{4,6},{6,0},{1,3},{3,5},{5,7},{7,1},{8,10},{10,12},{12... | collective-permute-start | bytes 3538952 | tf_op jit(solution)/shard_map/ppermute | solution.py:59
  44.9 56.5 %collective-permute-start.1 = (bf16[3,256,768]{2,1,0:T(8,128)(2,1)}, bf16[3,256,768]{2,1,0:T(8,128)(2,1)}, u32[]{:S(2)}, u32[]{:S(2)}) collective-permute-start(bf16[3,256,768]{2,1,0:T(8,128)(2,1)} %collective-permute-done), channel_id=1, source_target_pairs={{0,2},{2,4},{4,6},{6,0},{1,3},{3,5},{5,7},{7,1},{8,10},{10,12},{12... | collective-permute-start | bytes 3538952 | tf_op jit(solution)/shard_map/ppermute | solution.py:59
  45.7 58.5 %collective-permute-start.2 = (bf16[3,256,768]{2,1,0:T(8,128)(2,1)}, bf16[3,256,768]{2,1,0:T(8,128)(2,1)}, u32[]{:S(2)}, u32[]{:S(2)}) collective-permute-start(bf16[3,256,768]{2,1,0:T(8,128)(2,1)} %pad_maximum_fusion.2), channel_id=1, source_target_pairs={{0,6},{2,0},{4,2},{6,4},{1,7},{3,1},{5,3},{7,5},{8,14},{10,8},{12,... | collective-permute-start | bytes 3538952 | tf_op jit(solution)/shard_map/ppermute | solution.py:61
  141.7 23.8 %copy-start.11 = (bf16[3,256,768]{2,1,0:T(8,128)(2,1)S(1)}, bf16[3,256,768]{2,1,0:T(8,128)(2,1)}, u32[]{:S(2)}) copy-start(bf16[3,256,768]{2,1,0:T(8,128)(2,1)} %param.9) | copy-start | bytes 3538948
  144.5 64.2 %all-reduce.10.cloned.1.call-start = ((), (), s32[]{:S(2)}) async-start(), calls=%async_computation.8 | async-start | bytes 2359296 | tf_op jit(solution)/shard_map/psum | solution.py:143
  168.0 15.1 %copy-start.2 = (f32[768,768]{1,0:T(8,128)}, f32[768,768]{1,0:T(8,128)S(1)}, u32[]{:S(2)}) copy-start(f32[768,768]{1,0:T(8,128)S(1)} %get-tuple-element.134) | copy-start | bytes 7077892
  168.0 16.5 %copy-start.36 = (bf16[1536,768]{1,0:T(8,128)(2,1)S(1)}, bf16[1536,768]{1,0:T(8,128)(2,1)}, u32[]{:S(2)}) copy-start(bf16[1536,768]{1,0:T(8,128)(2,1)} %param.14) | copy-start | bytes 7077892
  184.5 24.2 %copy-start.32 = (f32[768]{0:T(1024)S(1)}, f32[768]{0:T(1024)}, u32[]{:S(2)}) copy-start(f32[768]{0:T(1024)} %get-tuple-element.119) | copy-start | bytes 9220
  187.5 61.0 %all-reduce.12.cloned.1.call-start = ((), (), s32[]{:S(2)}) async-start(), calls=%async_computation.9 | async-start | bytes 2359296 | tf_op jit(solution)/shard_map/psum | solution.py:158
  216.4 32.2 %copy-start.27 = (f32[768]{0:T(1024)}, f32[768]{0:T(1024)S(1)}, u32[]{:S(2)}) copy-start(f32[768]{0:T(1024)S(1)} %negate_multiply_fusion.2) | copy-start | bytes 9220
  227.4 138.2 %reduce-scatter.14.cloned.1.call-start = ((), (), s32[]{:S(2)}) async-start(), calls=%async_computation.10 | async-start | bytes 5898240 | tf_op jit(solution)/shard_map/reduce_scatter | solution.py:196
  256.4 16.9 %slice-start = ((s8[4718592]{0:T(1024)(128)(4,1)}), s8[524288]{0:T(1024)(128)(4,1)S(1)}, s32[]{:S(2)}) async-start(s8[4718592]{0:T(1024)(128)(4,1)} %bitcast.157), calls=%async_computation.19 | async-start | bytes 1048576
  260.8 12.5 %slice-start.1 = ((s8[4718592]{0:T(1024)(128)(4,1)}), s8[4194304]{0:T(1024)(128)(4,1)S(1)}, s32[]{:S(2)}) async-start(s8[4718592]{0:T(1024)(128)(4,1)} %bitcast.157), calls=%async_computation.20 | async-start | bytes 8388608
  307.2 103.4 %reduce-scatter.22.cloned.1.call-start = ((), (), s32[]{:S(2)}) async-start(), calls=%async_computation.15 | async-start | bytes 2211840
  378.0 61.2 %reduce-scatter.16.cloned.1.call-start = ((), (), s32[]{:S(2)}) async-start(), calls=%async_computation.12 | async-start | bytes 737280 | tf_op jit(solution)/shard_map/reduce_scatter | solution.py:222
  381.4 98.3 %reduce-scatter.20.cloned.1.call-start = ((), (), s32[]{:S(2)}) async-start(), calls=%async_computation.14 | async-start | bytes 2949120 | tf_op jit(solution)/shard_map/reduce_scatter | solution.py:228
  387.4 132.8 %reduce-scatter.18.cloned.1.call-start = ((), (), s32[]{:S(2)}) async-start(), calls=%async_computation.13 | async-start | bytes 2949120 | tf_op jit(solution)/shard_map/reduce_scatter | solution.py:225
  394.2 153.4 %reduce-scatter.24.cloned.1.call-start = ((), (), s32[]{:S(2)}) async-start(), calls=%async_computation.16 | async-start | bytes 245760
  398.0 176.8 %reduce-scatter.26.cloned.1.call-start = ((), (), s32[]{:S(2)}) async-start(), calls=%async_computation.17 | async-start | bytes 245760
  398.9 198.6 %all-reduce.14.cloned.1.call-start = ((), (), s32[]{:S(2)}) async-start(), calls=%async_computation.11 | async-start | bytes 2359296 | tf_op jit(solution)/shard_map/psum | solution.py:215
  404.3 279.5 %all-reduce.16.cloned.1.call-start = ((), (), s32[]{:S(2)}) async-start(), calls=%async_computation.18 | async-start | bytes 3833856 | tf_op jit(solution)/shard_map/psum | solution.py:245
  (33 other events, 107.9 us)
Sparse Core Ops, SparseCore 0:
  144.6 20.8 all-reduce.7
  187.7 20.9 all-reduce.9
  227.6 20.9 all-reduce.11
  307.3 58.2 reduce-scatter.13
  378.2 32.4 reduce-scatter.21
  414.2 25.0 reduce-scatter.15
  442.3 37.3 reduce-scatter.19
  482.8 37.3 reduce-scatter.17
  523.6 23.9 reduce-scatter.23
  550.8 23.9 reduce-scatter.25
  577.7 19.7 all-reduce.13
  600.8 82.8 all-reduce.15
